TPU v7x, 32 devices: a whole 2x2x4 slice. The times are simulated.
32 devices in a mesh: section: 4 (over x, core), shard: 4 (over z), replica: 2 (over y).
Axes of the slice: x: 2, y: 2, z: 4, core: 2. Of those that a mesh axis runs over, the one named last changes fastest.
Arguments:
- normed: bfloat16 [4, 2, 1024, 4096], P('section', None, ('shard', 'replica')), may hold values from -0.125 to 0.125
- key_cotangent: bfloat16 [4, 2, 1024, 512], P('section', None, ('shard', 'replica')), may hold values from -12 to 12
- positions: int32 [2, 1024], P(None, ('shard', 'replica')), may hold values from 0 to 1023, as said below
- key_weight: bfloat16 [4, 4096, 512], P('section', 'shard'), may hold values from -0.09375 to 0.09375
Outputs:
- key_weight_grad: bfloat16 [4, 4096, 512], P('section', 'shard')
- passed_grad: bfloat16 [4, 2, 1024, 4096], P('section', None, ('shard', 'replica'))
Inputs may be any that keep to these rules, and one draw needn't show every extreme that they name: `positions`: each token's position within its document of the micro-batch; in every micro-batch a document begins at every multiple of 1024 tokens, and in all but the first micro-batch at further places drawn at random.
All inputs are finite; a program needn't handle non-finite values.
Results may differ from a plain program's by a relative error of at most 0.018.
Values may be sent and summed in bfloat16 or wider, within the bound.
No kernel may reach another device: no remote copies, remote signals or barrier semaphores. Data moves between devices by JAX's collectives and lax.ppermute only.
A program may use at most 64 MiB of HBM per device.

v0:
```python
import jax
import jax.numpy as jnp
from jax import lax
from jax.sharding import PartitionSpec as P

HEAD = 128


def shifted(value, axis, steps):
    count = lax.axis_size(axis)
    leading, last = (max(0, -steps), min(count, count - steps))
    return lax.ppermute(value, axis, [(source, source + steps) for source in range(leading, last)])


def undo_rotation(cotangent, positions):
    half = HEAD // 2
    heads = cotangent.shape[-1] // HEAD
    index = jnp.arange(half, dtype=jnp.float32)
    freq = jnp.power(jnp.float32(500000.0), -2.0 * index / HEAD)
    angle = positions.astype(jnp.float32)[..., None] * freq
    angle = jnp.concatenate([angle, angle], axis=-1)[:, :, None, :]
    cosine = jnp.cos(angle)
    sine = jnp.sin(angle)
    lead = cotangent.shape[:2]
    grads = cotangent.astype(jnp.float32).reshape(lead + (heads, HEAD))
    swapped = jnp.concatenate([grads[..., half:], -grads[..., :half]], axis=-1)
    result = grads * cosine + swapped * sine
    return result.reshape(lead + (heads * HEAD,)).astype(jnp.bfloat16)


def per_device(normed, key_cotangent, positions, key_weight):
    key_grad = undo_rotation(key_cotangent[0], positions)
    width = normed.shape[3]
    local_rows = key_weight[0]
    partial_cols = jnp.einsum(
        "mtk,dk->mtd",
        lax.all_gather(key_grad, "shard", axis=1, tiled=True),
        local_rows,
        preferred_element_type=jnp.float32,
    ).astype(jnp.bfloat16)
    moved = lax.all_to_all(partial_cols, "shard", split_axis=1, concat_axis=2, tiled=True)
    input_grad = moved[:, :, :width][None]
    passed = shifted(input_grad, "section", -1)
    steps_tok = normed.shape[1] * normed.shape[2]
    flat_in = normed[0].reshape(steps_tok, width)
    flat_key = key_grad.reshape(steps_tok, key_grad.shape[-1])
    padding = lax.axis_size("shard") * local_rows.shape[0] - width
    padded = jnp.pad(flat_in, ((0, 0), (0, padding)))
    shard_total = lax.psum_scatter(
        lax.dot_general(
            padded, flat_key, (((0,), (0,)), ((), ())), preferred_element_type=jnp.float32
        ).astype(jnp.bfloat16),
        "shard",
        scatter_dimension=0,
        tiled=True,
    )
    shard_round = lax.optimization_barrier(shard_total).astype(jnp.float32)
    total = lax.psum(shard_round.astype(jnp.bfloat16), "replica")
    return (total[None], passed)


def solution(mesh):
    in_specs = (
        P("section", None, ("shard", "replica"), None),
        P("section", None, ("shard", "replica"), None),
        P(None, ("shard", "replica")),
        P("section", "shard", None),
    )
    out_specs = (P("section", "shard", None), P("section", None, ("shard", "replica"), None))
    return jax.shard_map(
        per_device, mesh=mesh, in_specs=in_specs, out_specs=out_specs, check_vma=False
    )
```

profile of v0, /device:TPU:0, one launch (start us, length us, event | category | flops | bytes accessed | tf_op | source)
XLA Modules:
  0.0 222.6 jit_solution(9915633863694696768)
XLA Ops:
  7.2 0.0 copy-start
  7.2 0.0 all-gather.2.cloned.1.call-start
  7.2 1.3 reshape.72
  8.5 0.7 convert_element_type.52
  9.2 0.1 broadcast_multiply_fusion
  9.3 0.5 fusion.6
  9.8 0.4 fusion.8
  10.2 0.5 add_convert_fusion
  10.7 0.2 mul.71
  10.9 0.9 mul.65
  11.8 1.3 mul.69
  13.0 1.8 fusion.3
  14.8 0.0 all-gather.2.cloned.1.call-update
  14.9 0.0 reduce-scatter.2.cloned.1.call-start
  14.9 0.0 copy-done
  14.9 3.2 %fusion = bf16[4096,512]{0,1:T(8,128)(2,1)} fusion(bf16[256,4096]{1,0:T(8,128)(2,1)S(1)} %bitcast.26, bf16[32,8,4,128]{3,2,1,0:T(4,128)(2,1)S(1)} %bitcast.28), kind=kOutput, calls=%fused_computation.1 | convolution fusion | flops 1075838976 | bytes 6553600 | tf_op jit(solution)/shard_map/dot_general | solution.py:50
  18.2 0.0 reduce-scatter.2.cloned.1.call-update
  18.2 0.0 all-reduce.2.cloned.1.call-start
  18.2 27.5 %all-gather.2.cloned.1.call-done = bf16[2,512,512]{2,1,0:T(8,128)(2,1)} async-done(((bf16[2,128,512]{2,1,0:T(8,128)(2,1)}), bf16[2,512,512]{2,1,0:T(8,128)(2,1)}) %all-gather.2.cloned.1.call-update) | async-done | bytes 1048592 | tf_op jit(solution)/shard_map/all_gather | solution.py:37
  45.7 0.0 copy-done.1
  45.7 2.5 %convolution_convert_fusion.1 = bf16[2,512,1024]{2,1,0:T(8,128)(2,1)S(1)} fusion(bf16[2,512,512]{2,1,0:T(8,128)(2,1)} %all-gather.2.cloned.1.call-done, bf16[1,1024,512]{2,1,0:T(8,128)(2,1)S(1)} %copy-done.1), kind=kOutput, calls=%fused_computation.2 | convolution fusion | flops 1074790400 | bytes 4194304 | tf_op jit(solution)/shard_map/mtk,dk->mtd/dot_general | solution.py:35
  48.2 2.2 copy.8
  50.4 107.6 %all_to_all.15 = bf16[2,512,1024]{2,0,1:T(2,128)(2,1)S(1)} all-to-all(bf16[2,512,1024]{2,0,1:T(2,128)(2,1)S(1)} %copy.8), channel_id=1, replica_groups=mesh['section'=4,'shard'=4,'replica'=2] {'shard'}, dimensions={1} | all-to-all | bytes 4194304 | tf_op jit(solution)/shard_map/all_to_all | solution.py:41
  158.0 2.9 %copy.9 = bf16[2,128,4,1024]{3,2,1,0:T(4,128)(2,1)} copy(bf16[2,128,4,1024]{3,0,1,2:T(2,128)(2,1)S(1)} %bitcast.27) | data formatting | bytes 4194304 | tf_op jit(solution)/shard_map/all_to_all | solution.py:41
  161.0 4.5 %broadcast_in_dim.10 = bf16[1,2,128,4096]{3,2,1,0:T(8,128)(2,1)} reshape(bf16[2,128,4,1024]{3,2,1,0:T(4,128)(2,1)} %copy.9) | data formatting | bytes 4194304 | tf_op jit(solution)/shard_map/broadcast_in_dim | solution.py:42
  165.5 1.3 collective-permute-start
  166.8 0.0 reduce-scatter.2.cloned.1.call-done
  166.8 0.0 all-reduce.2.cloned.1.call-update
  166.9 5.0 %collective-permute-done = bf16[1,2,128,4096]{3,2,1,0:T(8,128)(2,1)} collective-permute-done((bf16[1,2,128,4096]{3,2,1,0:T(8,128)(2,1)}, bf16[1,2,128,4096]{3,2,1,0:T(8,128)(2,1)}, u32[]{:S(2)}, u32[]{:S(2)}) %collective-permute-start) | collective-permute-done | bytes 2097184 | tf_op jit(solution)/shard_map/ppermute | solution.py:12
  171.9 38.7 %all-reduce.2.cloned.1.call-done = bf16[1,1024,512]{1,2,0:T(8,128)(2,1)} async-done(((bf16[1,1024,512]{1,2,0:T(8,128)(2,1)}), bf16[1,1024,512]{1,2,0:T(8,128)(2,1)}) %all-reduce.2.cloned.1.call-update) | async-done | bytes 1048592 | tf_op jit(solution)/shard_map/psum | solution.py:58
  210.6 2.3 %copy.10 = bf16[1,1024,512]{2,1,0:T(8,128)(2,1)} copy(bf16[1,1024,512]{1,2,0:T(8,128)(2,1)} %all-reduce.2.cloned.1.call-done) | data formatting | bytes 2097152
  212.9 3.1 %copy.18 = bf16[1,2,128,4096]{3,2,1,0:T(8,128)(2,1)} copy(bf16[1,2,128,4096]{3,2,1,0:T(8,128)(2,1)} %collective-permute-done) | data formatting | bytes 4194304
  (2 shorter events, 0.0 us)
Async XLA Ops:
  7.2 7.7 %copy-start = (bf16[1,2,128,4096]{3,2,1,0:T(8,128)(2,1)S(1)}, bf16[1,2,128,4096]{3,2,1,0:T(8,128)(2,1)}, u32[]{:S(2)}) copy-start(bf16[1,2,128,4096]{3,2,1,0:T(8,128)(2,1)} %param.4) | copy-start | bytes 6291460
  7.2 38.5 %all-gather.2.cloned.1.call-start = ((), (), s32[]{:S(2)}) async-start(), calls=%async_computation.4 | async-start | bytes 1310720 | tf_op jit(solution)/shard_map/all_gather | solution.py:37
  14.9 152.0 %reduce-scatter.2.cloned.1.call-start = ((), (), s32[]{:S(2)}) async-start(), calls=%async_computation.2 | async-start | bytes 5242880 | tf_op jit(solution)/shard_map/reduce_scatter | solution.py:49
  18.2 27.6 %copy-start.1 = (bf16[1,1024,512]{2,1,0:T(8,128)(2,1)S(1)}, bf16[1,1024,512]{2,1,0:T(8,128)(2,1)}, u32[]{:S(2)}) copy-start(bf16[1,1024,512]{2,1,0:T(8,128)(2,1)} %param.7) | copy-start | bytes 3145732
  18.2 192.5 %all-reduce.2.cloned.1.call-start = ((), (), s32[]{:S(2)}) async-start(), calls=%async_computation.3 | async-start | bytes 2097152 | tf_op jit(solution)/shard_map/psum | solution.py:58
  165.5 6.4 %collective-permute-start = (bf16[1,2,128,4096]{3,2,1,0:T(8,128)(2,1)}, bf16[1,2,128,4096]{3,2,1,0:T(8,128)(2,1)}, u32[]{:S(2)}, u32[]{:S(2)}) collective-permute-start(bf16[1,2,128,4096]{3,2,1,0:T(8,128)(2,1)} %broadcast_in_dim.10), channel_id=1, source_target_pairs={{8,0},{16,8},{24,16},{9,1},{17,9},{25,17},{10,2},{18,10},{26,18},{... | collective-permute-start | bytes 6291464 | tf_op jit(solution)/shard_map/ppermute | solution.py:12
Sparse Core Ops, SparseCore 0:
  15.0 30.6 all-gather.1
  48.0 115.0 reduce-scatter.1
  167.0 43.6 all-reduce.1
where the time goes:
time: 223 us
  blocking collectives  108 us (48%)
  waiting for transfers between devices  71.4 us (32%)
  local copies, waits for them, and re-layouts  18.6 us (8%)
  between operations  13.8 us (6%)
  matrix products  5.74 us (3%)
  other arithmetic  3.96 us (2%)
    all_to_all x1, blocking collectives, per_device(): lax.all_to_all(partial_cols, 'shard', split_axis=1, concat_axis=2, tiled=...  108 us
    psum x1, waiting for transfers between devices, per_device(): total = lax.psum(shard_round.astype(jnp.bfloat16), 'replica')  38.7 us
    all_gather x1, waiting for transfers between devices, per_device(): lax.all_gather(key_grad, 'shard', axis=1, tiled=True)  27.5 us
    unnamed x6, local copies, waits for them, and re-layouts  5.41 us
    ppermute x1, waiting for transfers between devices, shifted(): lax.ppermute(value, axis, [(source, source + steps) for source in range(l...  5.04 us
    broadcast_in_dim x1, local copies, waits for them, and re-layouts, per_device(): input_grad = moved[:, :, :width][None]  4.53 us
  transfers between devices with their start and end apart: 4, of which 3 were waited for; matrix products, arithmetic and copies ran while one was open for 7% of the time, Pallas kernels for 0%

commit v1 on v0

--- a/solution.py
+++ b/solution.py
@@ -4,6 +4,28 @@
 from jax.sharding import PartitionSpec as P
 
 HEAD = 128
+
+
+def cut_along(shard, dim, size):
+    before, after = (shard.shape[:dim], shard.shape[dim + 1 :])
+    return jnp.moveaxis(shard.reshape(*before, size, -1, *after), dim, 0)
+
+
+def in_order(parts, dim):
+    parts = jnp.moveaxis(parts, 0, dim)
+    shape = parts.shape
+    return parts.reshape(*shape[:dim], shape[dim] * shape[dim + 1], *shape[dim + 2 :])
+
+
+def exchange_in_pairs(x, axis, split_dim, concat_dim):
+    size, place = (lax.axis_size(axis), lax.axis_index(axis))
+    blocks = cut_along(x, split_dim, size)
+    gathered = [blocks[place]]
+    for turn in range(1, size):
+        sent = blocks[place ^ turn]
+        gathered.append(lax.ppermute(sent, axis, [(i, i ^ turn) for i in range(size)]))
+    blocks = jnp.stack(gathered)[place ^ jnp.arange(size)]
+    return in_order(blocks, concat_dim)
 
 
 def shifted(value, axis, steps):
@@ -38,7 +60,7 @@
         local_rows,
         preferred_element_type=jnp.float32,
     ).astype(jnp.bfloat16)
-    moved = lax.all_to_all(partial_cols, "shard", split_axis=1, concat_axis=2, tiled=True)
+    moved = exchange_in_pairs(partial_cols, "shard", 1, 2)
     input_grad = moved[:, :, :width][None]
     passed = shifted(input_grad, "section", -1)
     steps_tok = normed.shape[1] * normed.shape[2]

time: 223 us -> 215 us (0.964)
  blocking collectives: 108 us -> 0 us
  waiting for transfers between devices: 71.4 us -> 166 us
  starting transfers between devices: 1.4 us -> 5.85 us
    all_to_all x1 -> x0, blocking collectives: 108 us -> none  [per_device(): lax.all_to_all(partial_cols, 'shard', split_axis=1, concat_axis=2, tiled=...]
    ppermute x0 -> x3, waiting for transfers between devices: none -> 99.2 us  [exchange_in_pairs(): lax.ppermute(sent, axis, [(i, i ^ turn) for i in range(size)])]
    broadcast_in_dim x1 -> x0, local copies, waits for them, and re-layouts: 4.53 us -> none  [per_device(): input_grad = moved[:, :, :width][None]]
    psum x1, waiting for transfers between devices: 38.7 us -> 34.3 us  [per_device(): total = lax.psum(shard_round.astype(jnp.bfloat16), 'replica')]
    ppermute x0 -> x3, starting transfers between devices: none -> 4.45 us  [exchange_in_pairs(): lax.ppermute(sent, axis, [(i, i ^ turn) for i in range(size)])]
    transpose x0 -> x1, local copies, waits for them, and re-layouts: none -> 3.96 us  [in_order(): parts = jnp.moveaxis(parts, 0, dim)]
    gather x0 -> x1, local copies, waits for them, and re-layouts: none -> 3.66 us  [exchange_in_pairs(): blocks = jnp.stack(gathered)[place ^ jnp.arange(size)]]
    all_to_all x1 -> x0, local copies, waits for them, and re-layouts: 2.94 us -> none  [per_device(): lax.all_to_all(partial_cols, 'shard', split_axis=1, concat_axis=2, tiled=...]
  transfers between devices with their start and end apart: 4 -> 7, of which waited for: 3 -> 5; matrix products, arithmetic and copies ran while one was open for 7% -> 9% of each run, Pallas kernels for 0% -> 0%
where the time goes in v1:
time: 215 us
  waiting for transfers between devices  166 us (77%)
  local copies, waits for them, and re-layouts  17.8 us (8%)
  between operations  13.9 us (6%)
  starting transfers between devices  5.85 us (3%)
  matrix products  5.74 us (3%)
  other arithmetic  5.56 us (3%)
    ppermute x3, waiting for transfers between devices, exchange_in_pairs(): lax.ppermute(sent, axis, [(i, i ^ turn) for i in range(size)])  99.2 us
    psum x1, waiting for transfers between devices, per_device(): total = lax.psum(shard_round.astype(jnp.bfloat16), 'replica')  34.3 us
    all_gather x1, waiting for transfers between devices, per_device(): lax.all_gather(key_grad, 'shard', axis=1, tiled=True)  27.5 us
    unnamed x6, local copies, waits for them, and re-layouts  6.36 us
    ppermute x1, waiting for transfers between devices, shifted(): lax.ppermute(value, axis, [(source, source + steps) for source in range(l...  5.04 us
    ppermute x3, starting transfers between devices, exchange_in_pairs(): lax.ppermute(sent, axis, [(i, i ^ turn) for i in range(size)])  4.45 us
  transfers between devices with their start and end apart: 7, of which 5 were waited for; matrix products, arithmetic and copies ran while one was open for 9% of the time, Pallas kernels for 0%

profile of v1, /device:TPU:0, one launch (start us, length us, event | category | flops | bytes accessed | tf_op | source)
XLA Modules:
  0.0 214.9 jit_solution(2565810114340745589)
XLA Ops:
  7.2 0.0 all-gather.2.cloned.1.call-start
  7.2 1.3 reshape.98
  8.5 0.7 convert_element_type.52
  9.2 0.1 broadcast_multiply_fusion
  9.3 0.5 fusion.6
  9.8 0.4 fusion.9
  10.2 0.5 add_convert_fusion
  10.7 0.2 mul.71
  10.9 0.9 mul.65
  11.8 1.3 mul.69
  13.0 1.8 fusion.3
  14.9 0.0 reduce-scatter.2.cloned.1.call-start
  14.9 3.2 %fusion = bf16[4096,512]{0,1:T(8,128)(2,1)} fusion(bf16[256,4096]{1,0:T(8,128)(2,1)S(1)} %bitcast.39, bf16[32,8,4,128]{3,2,1,0:T(4,128)(2,1)S(1)} %bitcast.43), kind=kOutput, calls=%fused_computation.2 | convolution fusion | flops 1075838976 | bytes 6553600 | tf_op jit(solution)/shard_map/dot_general | solution.py:72
  18.2 0.0 all-reduce.2.cloned.1.call-start
  18.2 27.5 %all-gather.2.cloned.1.call-done = bf16[2,512,512]{2,1,0:T(8,128)(2,1)} async-done(((bf16[2,128,512]{2,1,0:T(8,128)(2,1)}), bf16[2,512,512]{2,1,0:T(8,128)(2,1)}) %all-gather.2.cloned.1.call-update) | async-done | bytes 1048592 | tf_op jit(solution)/shard_map/all_gather | solution.py:59
  45.7 2.5 %convolution_convert_fusion.1 = bf16[2,512,1024]{2,1,0:T(8,128)(2,1)S(1)} fusion(bf16[2,512,512]{2,1,0:T(8,128)(2,1)} %all-gather.2.cloned.1.call-done, bf16[1,1024,512]{2,1,0:T(8,128)(2,1)S(1)} %copy-done.1), kind=kOutput, calls=%fused_computation.4 | convolution fusion | flops 1074790400 | bytes 4194304 | tf_op jit(solution)/shard_map/mtk,dk->mtd/dot_general | solution.py:57
  48.2 0.2 dynamic-slice_bitcast_fusion.3
  48.5 1.9 collective-permute-start.2
  50.3 1.1 collective-permute-start.1
  51.4 1.5 collective-permute-start
  52.9 20.2 %collective-permute-done.2 = bf16[2,128,1024]{2,1,0:T(8,128)(2,1)S(1)} collective-permute-done((bf16[2,128,1024]{2,1,0:T(8,128)(2,1)S(1)}, bf16[2,128,1024]{2,1,0:T(8,128)(2,1)S(1)}, u32[]{:S(2)}, u32[]{:S(2)}) %collective-permute-start.2) | collective-permute-done | bytes 524320 | tf_op jit(solution)/shard_map/ppermute | solution.py:26
  73.1 79.0 %collective-permute-done.1 = bf16[2,128,1024]{2,1,0:T(8,128)(2,1)S(1)} collective-permute-done((bf16[2,128,1024]{2,1,0:T(8,128)(2,1)S(1)}, bf16[2,128,1024]{2,1,0:T(8,128)(2,1)S(1)}, u32[]{:S(2)}, u32[]{:S(2)}) %collective-permute-start.1) | collective-permute-done | bytes 524320 | tf_op jit(solution)/shard_map/ppermute | solution.py:26
  152.1 1.6 pad_maximum_fusion
  153.7 3.7 %gather_fusion = bf16[4,2,128,1024]{3,2,1,0:T(8,128)(2,1)} fusion(bf16[4,2,128,1024]{3,2,1,0:T(8,128)(2,1)} %pad_maximum_fusion, s32[1024]{0:T(1024)S(1)} %pad_clamp_fusion), kind=kCustom, calls=%fused_computation | custom fusion | bytes 4194320 | tf_op jit(solution)/shard_map/gather | solution.py:27
  157.4 4.0 %copy.8 = bf16[2,128,4,1024]{1,3,2,0:T(8,128)(2,1)} copy(bf16[2,128,4,1024]{3,1,0,2:T(8,128)(2,1)} %bitcast.40) | data formatting | bytes 4194304 | tf_op jit(solution)/shard_map/transpose | solution.py:15
  161.3 1.3 collective-permute-start.3
  162.6 0.0 reduce-scatter.2.cloned.1.call-done
  162.7 0.0 all-reduce.2.cloned.1.call-update
  162.7 5.0 %collective-permute-done.3 = bf16[1,2,128,4096]{2,3,1,0:T(8,128)(2,1)} collective-permute-done((bf16[1,2,128,4096]{2,3,1,0:T(8,128)(2,1)}, bf16[1,2,128,4096]{2,3,1,0:T(8,128)(2,1)}, u32[]{:S(2)}, u32[]{:S(2)}) %collective-permute-start.3) | collective-permute-done | bytes 2097184 | tf_op jit(solution)/shard_map/ppermute | solution.py:34
  167.7 4.1 %copy.10 = bf16[1,2,128,4096]{3,2,1,0:T(8,128)(2,1)} copy(bf16[1,2,128,4096]{2,3,1,0:T(8,128)(2,1)} %collective-permute-done.3) | data formatting | bytes 4194304
  171.8 34.3 %all-reduce.2.cloned.1.call-done = bf16[1,1024,512]{1,2,0:T(8,128)(2,1)} async-done(((bf16[1,1024,512]{1,2,0:T(8,128)(2,1)}), bf16[1,1024,512]{1,2,0:T(8,128)(2,1)}) %all-reduce.2.cloned.1.call-update) | async-done | bytes 1048592 | tf_op jit(solution)/shard_map/psum | solution.py:80
  206.1 2.3 %copy.9 = bf16[1,1024,512]{2,1,0:T(8,128)(2,1)} copy(bf16[1,1024,512]{1,2,0:T(8,128)(2,1)} %all-reduce.2.cloned.1.call-done) | data formatting | bytes 2097152
  (10 shorter events, 0.1 us)
Async XLA Ops:
  7.2 7.7 %copy-start = (bf16[1,2,128,4096]{3,2,1,0:T(8,128)(2,1)S(1)}, bf16[1,2,128,4096]{3,2,1,0:T(8,128)(2,1)}, u32[]{:S(2)}) copy-start(bf16[1,2,128,4096]{3,2,1,0:T(8,128)(2,1)} %param.4) | copy-start | bytes 6291460
  7.2 38.5 %all-gather.2.cloned.1.call-start = ((), (), s32[]{:S(2)}) async-start(), calls=%async_computation.3 | async-start | bytes 1310720 | tf_op jit(solution)/shard_map/all_gather | solution.py:59
  14.9 147.8 %reduce-scatter.2.cloned.1.call-start = ((), (), s32[]{:S(2)}) async-start(), calls=%async_computation.1 | async-start | bytes 5242880 | tf_op jit(solution)/shard_map/reduce_scatter | solution.py:71
  18.2 27.6 %copy-start.1 = (bf16[1,1024,512]{2,1,0:T(8,128)(2,1)S(1)}, bf16[1,1024,512]{2,1,0:T(8,128)(2,1)}, u32[]{:S(2)}) copy-start(bf16[1,1024,512]{2,1,0:T(8,128)(2,1)} %param.7) | copy-start | bytes 3145732
  18.2 187.9 %all-reduce.2.cloned.1.call-start = ((), (), s32[]{:S(2)}) async-start(), calls=%async_computation.2 | async-start | bytes 2097152 | tf_op jit(solution)/shard_map/psum | solution.py:80
  48.5 24.6 %collective-permute-start.2 = (bf16[2,128,1024]{2,1,0:T(8,128)(2,1)S(1)}, bf16[2,128,1024]{2,1,0:T(8,128)(2,1)S(1)}, u32[]{:S(2)}, u32[]{:S(2)}) collective-permute-start(bf16[2,128,1024]{2,1,0:T(8,128)(2,1)S(1)} %get-tuple-element.11), channel_id=1, source_target_pairs={{0,6},{2,4},{4,2},{6,0},{1,7},{3,5},{5,3},{7,1},{8,14},{10,12},{12... | collective-permute-start | bytes 1572872 | tf_op jit(solution)/shard_map/ppermute | solution.py:26
  50.3 101.8 %collective-permute-start.1 = (bf16[2,128,1024]{2,1,0:T(8,128)(2,1)S(1)}, bf16[2,128,1024]{2,1,0:T(8,128)(2,1)S(1)}, u32[]{:S(2)}, u32[]{:S(2)}) collective-permute-start(bf16[2,128,1024]{2,1,0:T(8,128)(2,1)S(1)} %get-tuple-element.12), channel_id=1, source_target_pairs={{0,4},{2,6},{4,0},{6,2},{1,5},{3,7},{5,1},{7,3},{8,12},{10,14},{12... | collective-permute-start | bytes 1572872 | tf_op jit(solution)/shard_map/ppermute | solution.py:26
  51.4 100.7 %collective-permute-start = (bf16[2,128,1024]{2,1,0:T(8,128)(2,1)S(1)}, bf16[2,128,1024]{2,1,0:T(8,128)(2,1)S(1)}, u32[]{:S(2)}, u32[]{:S(2)}) collective-permute-start(bf16[2,128,1024]{2,1,0:T(8,128)(2,1)S(1)} %get-tuple-element.13), channel_id=1, source_target_pairs={{0,2},{2,0},{4,6},{6,4},{1,3},{3,1},{5,7},{7,5},{8,10},{10,8},{12,... | collective-permute-start | bytes 1572872 | tf_op jit(solution)/shard_map/ppermute | solution.py:26
  161.3 6.4 %collective-permute-start.3 = (bf16[1,2,128,4096]{2,3,1,0:T(8,128)(2,1)}, bf16[1,2,128,4096]{2,3,1,0:T(8,128)(2,1)}, u32[]{:S(2)}, u32[]{:S(2)}) collective-permute-start(bf16[1,2,128,4096]{2,3,1,0:T(8,128)(2,1)} %bitcast.41), channel_id=1, source_target_pairs={{8,0},{16,8},{24,16},{9,1},{17,9},{25,17},{10,2},{18,10},{26,18},{... | collective-permute-start | bytes 6291464 | tf_op jit(solution)/shard_map/ppermute | solution.py:34
Sparse Core Ops, SparseCore 0:
  15.0 30.6 all-gather.1
  48.0 110.3 reduce-scatter.1
  162.8 43.2 all-reduce.1
